TPU v7x, 32 devices: a whole 2x2x4 slice. The times are simulated.
32 devices in a mesh: rows: 16 (over z, y, core), cent: 2 (over x).
Axes of the slice: x: 2, y: 2, z: 4, core: 2. Of those that a mesh axis runs over, the one named last changes fastest.
Arguments:
- vectors: bfloat16 [32768, 1024], P('rows'), may hold values from -40 to 40
- centroids: bfloat16 [1024, 4096], P('rows', 'cent'), may hold values from -8 to 8
Outputs:
- centroid_sums: float32 [1024, 4096], P('rows', 'cent')
All inputs are finite; a program needn't handle non-finite values.
Results may differ from a plain program's by a relative error of at most 0.0017.
Values may be sent and summed in bfloat16 or wider, within the bound.
A program may use at most 64 MiB of HBM per device.

v0:
```python
import math
import jax
import jax.numpy as jnp
from jax import lax
from jax.sharding import PartitionSpec as P

K = 4096
ITERS = 3
sharpness = 3.0


def on_device(vectors, centroids):
    row_count = vectors.shape[0]
    width = vectors.shape[1]
    window = vectors
    scores = jnp.dot(
        window,
        lax.all_gather(centroids, "rows", axis=0, tiled=True),
        preferred_element_type=jnp.float32,
    )
    scores = scores * (sharpness / math.sqrt(width))
    row_top = lax.pmax(jnp.max(scores, axis=1), "cent")
    numerator = jnp.exp(scores - row_top[:, None])
    row_total = lax.psum(jnp.sum(numerator, axis=1), "cent")
    balanced = numerator / row_total[:, None]
    target = row_count * lax.axis_size("rows") / K
    for iteration in range(ITERS):
        column_sum = jnp.sum(balanced, axis=0)
        column_mass = lax.psum(column_sum, "rows")
        column_scale = target / column_mass
        balanced = balanced * column_scale[None, :]
        row_mass = lax.psum(jnp.sum(balanced, axis=1), "cent")
        balanced = balanced / row_mass[:, None]
    weights = balanced.astype(jnp.bfloat16)
    factor = K / (row_count * lax.axis_size("rows"))
    window = vectors
    mine = lax.psum_scatter(
        lax.dot_general(
            window, weights, (((0,), (0,)), ((), ())), preferred_element_type=jnp.float32
        ),
        "rows",
        scatter_dimension=0,
        tiled=True,
    )
    return mine * factor


def solution(mesh):
    return jax.shard_map(
        on_device,
        mesh=mesh,
        in_specs=(P("rows", None), P("rows", "cent")),
        out_specs=P("rows", "cent"),
        check_vma=False,
    )
```

profile of v0, /device:TPU:0, one launch (start us, length us, event | category | flops | bytes accessed | tf_op | source)
XLA Modules:
  0.0 386.2 jit_solution(11446826470317669100)
XLA Ops:
  6.5 0.0 all-gather.2.cloned.1.call-start
  6.5 0.7 all-gather.2.cloned.1.call-update
  7.3 0.0 reduce-scatter.4.cloned.1.call-start
  7.3 55.3 %all-gather.2.cloned.1.call-done = bf16[1024,2048]{1,0:T(8,128)(2,1)} async-done(((bf16[64,2048]{1,0:T(8,128)(2,1)}), bf16[1024,2048]{1,0:T(8,128)(2,1)}) %all-gather.2.cloned.1.call-update) | async-done | bytes 4194320 | tf_op jit(solution)/shard_map/all_gather | solution.py:18
  62.6 15.2 %multiply_reduce_fusion.3 = (f32[2048]{0:T(1024)S(1)}, f32[2048,2048]{0,1:T(8,128)}) fusion(bf16[2048,1024]{1,0:T(8,128)(2,1)} %param.2, bf16[1024,2048]{1,0:T(8,128)(2,1)} %all-gather.2.cloned.1.call-done), kind=kOutput, calls=%fused_computation.7 | convolution fusion | flops 8598321152 | bytes 25174016 | tf_op jit(solution)/shard_map/dot_general | solution.py:16
  77.9 5.0 %pmax.7 = f32[2048]{0:T(1024)S(1)} all-reduce(f32[2048]{0:T(1024)S(1)} %get-tuple-element.7), channel_id=1, replica_groups=mesh['rows'=16,'cent'=2] {'cent'}, use_global_device_ids=true, to_apply=%region_1.0 | all-reduce | flops 2048 | bytes 16384 | tf_op jit(solution)/shard_map/pmax | solution.py:22
  82.8 8.5 %fusion.1 = f32[2048]{0:T(1024)S(1)} fusion(f32[2048,2048]{0,1:T(8,128)} %get-tuple-element.8, f32[2048]{0:T(1024)S(1)} %pmax.7), kind=kLoop, calls=%fused_computation.9 | loop fusion | flops 12580864 | bytes 16793600 | tf_op jit(solution)/shard_map/reduce_sum | solution.py:24
  91.4 5.0 %psum.49 = f32[2048]{0:T(1024)S(1)} all-reduce(f32[2048]{0:T(1024)S(1)} %fusion.1), channel_id=1, replica_groups=mesh['rows'=16,'cent'=2] {'cent'}, use_global_device_ids=true, to_apply=%region_3.0 | all-reduce | flops 2048 | bytes 16384 | tf_op jit(solution)/shard_map/psum | solution.py:24
  96.4 7.7 %fusion.4 = f32[2048]{0:T(1024)S(1)} fusion(f32[2048]{0:T(1024)S(1)} %psum.49, f32[2048]{0:T(1024)S(1)} %pmax.7, f32[2048,2048]{0,1:T(8,128)} %get-tuple-element.8), kind=kLoop, calls=%fused_computation.16 | loop fusion | flops 16775168 | bytes 16801792 | tf_op jit(solution)/shard_map/reduce_sum | solution.py:28
  104.1 30.0 %psum.50 = f32[2048]{0:T(1024)S(1)} all-reduce(f32[2048]{0:T(1024)S(1)} %fusion.4), channel_id=1, replica_groups=mesh['rows'=16,'cent'=2] {'rows'}, use_global_device_ids=true, to_apply=%region_5.0 | all-reduce | flops 2048 | bytes 16384 | tf_op jit(solution)/shard_map/psum | solution.py:29
  134.1 8.1 %multiply_reduce_fusion.2 = f32[2048]{0:T(1024)S(1)} fusion(f32[2048]{0:T(1024)S(1)} %broadcast_divide_fusion.2, f32[2048]{0:T(1024)S(1)} %psum.49, f32[2048]{0:T(1024)S(1)} %pmax.7, f32[2048,2048]{0,1:T(8,128)} %get-tuple-element.8), kind=kLoop, calls=%fused_computation.6 | loop fusion | flops 20969472 | bytes 16809984 | tf_op jit(solution)/shard_map/reduce_sum | solution.py:32
  142.2 5.0 %psum.51 = f32[2048]{0:T(1024)S(1)} all-reduce(f32[2048]{0:T(1024)S(1)} %multiply_reduce_fusion.2), channel_id=1, replica_groups=mesh['rows'=16,'cent'=2] {'cent'}, use_global_device_ids=true, to_apply=%region_7.0 | all-reduce | flops 2048 | bytes 16384 | tf_op jit(solution)/shard_map/psum | solution.py:32
  147.2 13.1 %fusion.6 = (f32[2048]{0:T(1024)S(1)}, f32[2048,2048]{0,1:T(8,128)}) fusion(f32[2048]{0:T(1024)S(1)} %psum.51, f32[2048]{0:T(1024)S(1)} %broadcast_divide_fusion.2, f32[2048]{0:T(1024)S(1)} %psum.49, f32[2048]{0:T(1024)S(1)} %pmax.7, f32[2048,2048]{0,1:T(8,128)} %get-tuple-element.8), kind=kLoop, calls=%fused_computation.18 | loop fusion | flops 25163776 | bytes 33595392 | tf_op jit(solution)/shard_map/reduce_sum | solution.py:28
  160.3 30.2 %psum.52 = f32[2048]{0:T(1024)S(1)} all-reduce(f32[2048]{0:T(1024)S(1)} %get-tuple-element.5), channel_id=1, replica_groups=mesh['rows'=16,'cent'=2] {'rows'}, use_global_device_ids=true, to_apply=%region_9.0 | all-reduce | flops 2048 | bytes 16384 | tf_op jit(solution)/shard_map/psum | solution.py:29
  190.5 6.9 %multiply_reduce_fusion.1 = f32[2048]{0:T(1024)S(1)} fusion(f32[2048,2048]{0,1:T(8,128)} %get-tuple-element.6, f32[2048]{0:T(1024)S(1)} %broadcast_divide_fusion.1), kind=kLoop, calls=%fused_computation.4 | loop fusion | flops 8386560 | bytes 16793600 | tf_op jit(solution)/shard_map/reduce_sum | solution.py:32
  197.4 5.0 %psum.53 = f32[2048]{0:T(1024)S(1)} all-reduce(f32[2048]{0:T(1024)S(1)} %multiply_reduce_fusion.1), channel_id=1, replica_groups=mesh['rows'=16,'cent'=2] {'cent'}, use_global_device_ids=true, to_apply=%region_11.0 | all-reduce | flops 2048 | bytes 16384 | tf_op jit(solution)/shard_map/psum | solution.py:32
  202.5 7.1 %fusion.5 = f32[2048]{0:T(1024)S(1)} fusion(f32[2048]{0:T(1024)S(1)} %psum.53, f32[2048,2048]{0,1:T(8,128)} %get-tuple-element.6, f32[2048]{0:T(1024)S(1)} %broadcast_divide_fusion.1), kind=kLoop, calls=%fused_computation.17 | loop fusion | flops 12580864 | bytes 16801792 | tf_op jit(solution)/shard_map/reduce_sum | solution.py:28
  209.6 30.0 %psum.54 = f32[2048]{0:T(1024)S(1)} all-reduce(f32[2048]{0:T(1024)S(1)} %fusion.5), channel_id=1, replica_groups=mesh['rows'=16,'cent'=2] {'rows'}, use_global_device_ids=true, to_apply=%region_13.0 | all-reduce | flops 2048 | bytes 16384 | tf_op jit(solution)/shard_map/psum | solution.py:29
  239.6 7.2 %multiply_reduce_fusion = f32[2048]{0:T(1024)S(1)} fusion(f32[2048]{0:T(1024)S(1)} %broadcast_divide_fusion, f32[2048]{0:T(1024)S(1)} %psum.53, f32[2048,2048]{0,1:T(8,128)} %get-tuple-element.6, f32[2048]{0:T(1024)S(1)} %broadcast_divide_fusion.1), kind=kLoop, calls=%fused_computation.2 | loop fusion | flops 16775168 | bytes 16809984 | tf_op jit(solution)/shard_map/reduce_sum | solution.py:32
  246.8 5.0 %psum.55 = f32[2048]{0:T(1024)S(1)} all-reduce(f32[2048]{0:T(1024)S(1)} %multiply_reduce_fusion), channel_id=1, replica_groups=mesh['rows'=16,'cent'=2] {'cent'}, use_global_device_ids=true, to_apply=%region_15.0 | all-reduce | flops 2048 | bytes 16384 | tf_op jit(solution)/shard_map/psum | solution.py:32
  251.8 15.7 %fusion.3 = f32[1024,2048]{0,1:T(8,128)} fusion(bf16[2048,1024]{1,0:T(8,128)(2,1)} %param.2, f32[2048]{0:T(1024)S(1)} %psum.55, f32[2048]{0:T(1024)S(1)} %broadcast_divide_fusion, f32[2048,2048]{0,1:T(8,128)} %get-tuple-element.6, f32[2048]{0:T(1024)S(1)} %psum.53, f32[2048]{0:T(1024)S(1)} %broadcast_divide_fusion.1), kind=kOutput, calls=%fused_computation.11 | convolution fusion | flops 8610906112 | bytes 29392896 | tf_op jit(solution)/shard_map/dot_general | solution.py:38
  267.5 9.1 %copy.6 = f32[1024,2048]{1,0:T(8,128)} copy(f32[1024,2048]{0,1:T(8,128)} %fusion.3) | data formatting | bytes 16777216
  276.6 0.0 reduce-scatter.4.cloned.1.call-update
  276.6 100.9 %reduce-scatter.4.cloned.1.call-done = f32[64,2048]{1,0:T(8,128)} async-done(((f32[1024,2048]{1,0:T(8,128)}), f32[64,2048]{1,0:T(8,128)}) %reduce-scatter.4.cloned.1.call-update) | async-done | bytes 524304 | tf_op jit(solution)/shard_map/reduce_scatter | solution.py:37
  377.5 1.9 broadcast_multiply_fusion
  (3 shorter events, 0.0 us)
Async XLA Ops:
  6.5 56.1 %all-gather.2.cloned.1.call-start = ((), (), s32[]{:S(2)}) async-start(), calls=%async_computation.1 | async-start | bytes 4456448 | tf_op jit(solution)/shard_map/all_gather | solution.py:18
  7.3 370.3 %reduce-scatter.4.cloned.1.call-start = ((), (), s32[]{:S(2)}) async-start(), calls=%async_computation.2 | async-start | bytes 8912896 | tf_op jit(solution)/shard_map/reduce_scatter | solution.py:37
Sparse Core Ops, SparseCore 0:
  9.5 53.0 all-gather.1
  276.7 100.7 reduce-scatter.3
where the time goes:
time: 387 us; the launch traced here: 386 us
  waiting for transfers between devices  157 us (41%)
  blocking collectives  115 us (30%)
  other arithmetic  60.6 us (16%)
  matrix products  30.9 us (8%)
  between operations  13.5 us (3%)
  local copies, waits for them, and re-layouts  9.11 us (2%)
    reduce_scatter x1, waiting for transfers between devices, on_device(): lax.psum_scatter(lax.dot_general(window, weights, (((0,), (0,)), ((), ())...  101 us
    psum x3, blocking collectives, on_device(): column_mass = lax.psum(column_sum, 'rows')  90.2 us
    all_gather x1, waiting for transfers between devices, on_device(): lax.all_gather(centroids, 'rows', axis=0, tiled=True)  55.3 us
    reduce_sum x3, other arithmetic, on_device(): column_sum = jnp.sum(balanced, axis=0)  27.9 us
    reduce_sum x3, other arithmetic, on_device(): row_mass = lax.psum(jnp.sum(balanced, axis=1), 'cent')  22.3 us
    dot_general x1, matrix products, on_device(): lax.dot_general(window, weights, (((0,), (0,)), ((), ())), preferred_elem...  15.7 us
    dot_general x1, matrix products, on_device(): jnp.dot(window, lax.all_gather(centroids, 'rows', axis=0, tiled=True), pr...  15.2 us
    psum x3, blocking collectives, on_device(): row_mass = lax.psum(jnp.sum(balanced, axis=1), 'cent')  15 us
  transfers between devices with their start and end apart: 2, of which 2 were waited for; matrix products, arithmetic and copies ran while one was open for 0% of the time, Pallas kernels for 0%

commit v1 on v0

--- a/solution.py
+++ b/solution.py
@@ -26,7 +26,7 @@
     target = row_count * lax.axis_size("rows") / K
     for iteration in range(ITERS):
         column_sum = jnp.sum(balanced, axis=0)
-        column_mass = lax.psum(column_sum, "rows")
+        column_mass = jnp.sum(lax.all_gather(column_sum, "rows"), axis=0)
         column_scale = target / column_mass
         balanced = balanced * column_scale[None, :]
         row_mass = lax.psum(jnp.sum(balanced, axis=1), "cent")

time: 387 us -> 353 us (0.912)
  blocking collectives: 115 us -> 81.2 us
    psum x3 -> x0, blocking collectives: 90.2 us -> none  [on_device(): column_mass = lax.psum(column_sum, 'rows')]
    all_gather x0 -> x3, blocking collectives: none -> 56.2 us  [on_device(): column_mass = jnp.sum(lax.all_gather(column_sum, 'rows'), axis=0)]
where the time goes in v1:
time: 353 us; the launch traced here: 352 us
  waiting for transfers between devices  157 us (44%)
  blocking collectives  81.2 us (23%)
  other arithmetic  60.7 us (17%)
  matrix products  30.9 us (9%)
  between operations  13.5 us (4%)
  local copies, waits for them, and re-layouts  9.19 us (3%)
    reduce_scatter x1, waiting for transfers between devices, on_device(): lax.psum_scatter(lax.dot_general(window, weights, (((0,), (0,)), ((), ())...  101 us
    all_gather x3, blocking collectives, on_device(): column_mass = jnp.sum(lax.all_gather(column_sum, 'rows'), axis=0)  56.2 us
    all_gather x1, waiting for transfers between devices, on_device(): lax.all_gather(centroids, 'rows', axis=0, tiled=True)  55.3 us
    reduce_sum x3, other arithmetic, on_device(): column_sum = jnp.sum(balanced, axis=0)  27.9 us
    reduce_sum x3, other arithmetic, on_device(): row_mass = lax.psum(jnp.sum(balanced, axis=1), 'cent')  22.3 us
    dot_general x1, matrix products, on_device(): lax.dot_general(window, weights, (((0,), (0,)), ((), ())), preferred_elem...  15.7 us
    dot_general x1, matrix products, on_device(): jnp.dot(window, lax.all_gather(centroids, 'rows', axis=0, tiled=True), pr...  15.2 us
    psum x3, blocking collectives, on_device(): row_mass = lax.psum(jnp.sum(balanced, axis=1), 'cent')  15 us
  transfers between devices with their start and end apart: 2, of which 2 were waited for; matrix products, arithmetic and copies ran while one was open for 0% of the time, Pallas kernels for 0%

profile of v1, /device:TPU:0, one launch (start us, length us, event | category | flops | bytes accessed | tf_op | source)
XLA Modules:
  0.0 352.4 jit_solution(1768674245567163976)
XLA Ops:
  6.5 0.0 all-gather.5.cloned.1.call-start
  6.5 0.7 all-gather.5.cloned.1.call-update
  7.3 0.0 reduce-scatter.4.cloned.1.call-start
  7.3 55.3 %all-gather.5.cloned.1.call-done = bf16[1024,2048]{1,0:T(8,128)(2,1)} async-done(((bf16[64,2048]{1,0:T(8,128)(2,1)}), bf16[1024,2048]{1,0:T(8,128)(2,1)}) %all-gather.5.cloned.1.call-update) | async-done | bytes 4194320 | tf_op jit(solution)/shard_map/all_gather | solution.py:18
  62.6 15.2 %multiply_reduce_fusion.3 = (f32[2048]{0:T(1024)S(1)}, f32[2048,2048]{0,1:T(8,128)}) fusion(bf16[2048,1024]{1,0:T(8,128)(2,1)} %param.2, bf16[1024,2048]{1,0:T(8,128)(2,1)} %all-gather.5.cloned.1.call-done), kind=kOutput, calls=%fused_computation.7 | convolution fusion | flops 8598321152 | bytes 25174016 | tf_op jit(solution)/shard_map/dot_general | solution.py:16
  77.9 5.0 %pmax.7 = f32[2048]{0:T(1024)S(1)} all-reduce(f32[2048]{0:T(1024)S(1)} %get-tuple-element.7), channel_id=1, replica_groups=mesh['rows'=16,'cent'=2] {'cent'}, use_global_device_ids=true, to_apply=%region_1.0 | all-reduce | flops 2048 | bytes 16384 | tf_op jit(solution)/shard_map/pmax | solution.py:22
  82.8 8.5 %fusion.1 = f32[2048]{0:T(1024)S(1)} fusion(f32[2048,2048]{0,1:T(8,128)} %get-tuple-element.8, f32[2048]{0:T(1024)S(1)} %pmax.7), kind=kLoop, calls=%fused_computation.9 | loop fusion | flops 12580864 | bytes 16793600 | tf_op jit(solution)/shard_map/reduce_sum | solution.py:24
  91.4 5.0 %psum.28 = f32[2048]{0:T(1024)S(1)} all-reduce(f32[2048]{0:T(1024)S(1)} %fusion.1), channel_id=1, replica_groups=mesh['rows'=16,'cent'=2] {'cent'}, use_global_device_ids=true, to_apply=%region_3.0 | all-reduce | flops 2048 | bytes 16384 | tf_op jit(solution)/shard_map/psum | solution.py:24
  96.4 7.7 %fusion.4 = f32[2048]{0:T(1024)S(1)} fusion(f32[2048]{0:T(1024)S(1)} %psum.28, f32[2048]{0:T(1024)S(1)} %pmax.7, f32[2048,2048]{0,1:T(8,128)} %get-tuple-element.8), kind=kLoop, calls=%fused_computation.16 | loop fusion | flops 16775168 | bytes 16801792 | tf_op jit(solution)/shard_map/reduce_sum | solution.py:28
  104.1 19.3 %all-gather = f32[32768]{0:T(1024)S(1)} all-gather(f32[2048]{0:T(1024)S(1)} %fusion.4), channel_id=2, replica_groups=mesh['rows'=16,'cent'=2] {'rows'}, dimensions={0}, use_global_device_ids=true | all-gather | bytes 139264 | tf_op jit(solution)/shard_map/all_gather | solution.py:29
  123.5 8.1 %multiply_reduce_fusion.2 = f32[2048]{0:T(1024)S(1)} fusion(f32[2048]{0:T(1024)S(1)} %broadcast_divide_fusion.2, f32[2048]{0:T(1024)S(1)} %psum.28, f32[2048]{0:T(1024)S(1)} %pmax.7, f32[2048,2048]{0,1:T(8,128)} %get-tuple-element.8), kind=kLoop, calls=%fused_computation.6 | loop fusion | flops 20969472 | bytes 16809984 | tf_op jit(solution)/shard_map/reduce_sum | solution.py:32
  131.6 5.0 %psum.29 = f32[2048]{0:T(1024)S(1)} all-reduce(f32[2048]{0:T(1024)S(1)} %multiply_reduce_fusion.2), channel_id=1, replica_groups=mesh['rows'=16,'cent'=2] {'cent'}, use_global_device_ids=true, to_apply=%region_7.0 | all-reduce | flops 2048 | bytes 16384 | tf_op jit(solution)/shard_map/psum | solution.py:32
  136.6 13.1 %fusion.6 = (f32[2048]{0:T(1024)S(1)}, f32[2048,2048]{0,1:T(8,128)}) fusion(f32[2048]{0:T(1024)S(1)} %psum.29, f32[2048]{0:T(1024)S(1)} %broadcast_divide_fusion.2, f32[2048]{0:T(1024)S(1)} %psum.28, f32[2048]{0:T(1024)S(1)} %pmax.7, f32[2048,2048]{0,1:T(8,128)} %get-tuple-element.8), kind=kLoop, calls=%fused_computation.18 | loop fusion | flops 25163776 | bytes 33595392 | tf_op jit(solution)/shard_map/reduce_sum | solution.py:28
  149.7 17.6 %all-gather.1 = f32[32768]{0:T(1024)S(1)} all-gather(f32[2048]{0:T(1024)S(1)} %get-tuple-element.5), channel_id=3, replica_groups=mesh['rows'=16,'cent'=2] {'rows'}, dimensions={0}, use_global_device_ids=true | all-gather | bytes 139264 | tf_op jit(solution)/shard_map/all_gather | solution.py:29
  167.4 6.9 %multiply_reduce_fusion.1 = f32[2048]{0:T(1024)S(1)} fusion(f32[2048,2048]{0,1:T(8,128)} %get-tuple-element.6, f32[2048]{0:T(1024)S(1)} %broadcast_divide_fusion.1), kind=kLoop, calls=%fused_computation.4 | loop fusion | flops 8386560 | bytes 16793600 | tf_op jit(solution)/shard_map/reduce_sum | solution.py:32
  174.3 5.0 %psum.30 = f32[2048]{0:T(1024)S(1)} all-reduce(f32[2048]{0:T(1024)S(1)} %multiply_reduce_fusion.1), channel_id=1, replica_groups=mesh['rows'=16,'cent'=2] {'cent'}, use_global_device_ids=true, to_apply=%region_11.0 | all-reduce | flops 2048 | bytes 16384 | tf_op jit(solution)/shard_map/psum | solution.py:32
  179.3 7.1 %fusion.5 = f32[2048]{0:T(1024)S(1)} fusion(f32[2048]{0:T(1024)S(1)} %psum.30, f32[2048,2048]{0,1:T(8,128)} %get-tuple-element.6, f32[2048]{0:T(1024)S(1)} %broadcast_divide_fusion.1), kind=kLoop, calls=%fused_computation.17 | loop fusion | flops 12580864 | bytes 16801792 | tf_op jit(solution)/shard_map/reduce_sum | solution.py:28
  186.5 19.3 %all-gather.2 = f32[32768]{0:T(1024)S(1)} all-gather(f32[2048]{0:T(1024)S(1)} %fusion.5), channel_id=4, replica_groups=mesh['rows'=16,'cent'=2] {'rows'}, dimensions={0}, use_global_device_ids=true | all-gather | bytes 139264 | tf_op jit(solution)/shard_map/all_gather | solution.py:29
  205.8 7.2 %multiply_reduce_fusion = f32[2048]{0:T(1024)S(1)} fusion(f32[2048]{0:T(1024)S(1)} %broadcast_divide_fusion, f32[2048]{0:T(1024)S(1)} %psum.30, f32[2048,2048]{0,1:T(8,128)} %get-tuple-element.6, f32[2048]{0:T(1024)S(1)} %broadcast_divide_fusion.1), kind=kLoop, calls=%fused_computation.2 | loop fusion | flops 16775168 | bytes 16809984 | tf_op jit(solution)/shard_map/reduce_sum | solution.py:32
  213.0 5.0 %psum.31 = f32[2048]{0:T(1024)S(1)} all-reduce(f32[2048]{0:T(1024)S(1)} %multiply_reduce_fusion), channel_id=1, replica_groups=mesh['rows'=16,'cent'=2] {'cent'}, use_global_device_ids=true, to_apply=%region_15.0 | all-reduce | flops 2048 | bytes 16384 | tf_op jit(solution)/shard_map/psum | solution.py:32
  218.0 15.7 %fusion.3 = f32[1024,2048]{0,1:T(8,128)} fusion(bf16[2048,1024]{1,0:T(8,128)(2,1)} %param.2, f32[2048]{0:T(1024)S(1)} %psum.31, f32[2048]{0:T(1024)S(1)} %broadcast_divide_fusion, f32[2048,2048]{0,1:T(8,128)} %get-tuple-element.6, f32[2048]{0:T(1024)S(1)} %psum.30, f32[2048]{0:T(1024)S(1)} %broadcast_divide_fusion.1), kind=kOutput, calls=%fused_computation.11 | convolution fusion | flops 8610906112 | bytes 29392896 | tf_op jit(solution)/shard_map/dot_general | solution.py:38
  233.7 9.1 %copy.7 = f32[1024,2048]{1,0:T(8,128)} copy(f32[1024,2048]{0,1:T(8,128)} %fusion.3) | data formatting | bytes 16777216
  242.8 0.0 reduce-scatter.4.cloned.1.call-update
  242.8 100.9 %reduce-scatter.4.cloned.1.call-done = f32[64,2048]{1,0:T(8,128)} async-done(((f32[1024,2048]{1,0:T(8,128)}), f32[64,2048]{1,0:T(8,128)}) %reduce-scatter.4.cloned.1.call-update) | async-done | bytes 524304 | tf_op jit(solution)/shard_map/reduce_scatter | solution.py:37
  343.7 1.9 broadcast_multiply_fusion
  (9 shorter events, 0.2 us)
Async XLA Ops:
  6.5 56.1 %all-gather.5.cloned.1.call-start = ((), (), s32[]{:S(2)}) async-start(), calls=%async_computation.1 | async-start | bytes 4456448 | tf_op jit(solution)/shard_map/all_gather | solution.py:18
  7.3 336.5 %reduce-scatter.4.cloned.1.call-start = ((), (), s32[]{:S(2)}) async-start(), calls=%async_computation.2 | async-start | bytes 8912896 | tf_op jit(solution)/shard_map/reduce_scatter | solution.py:37
Sparse Core Ops, SparseCore 0:
  9.5 53.0 all-gather.4
  242.9 100.7 reduce-scatter.3
